TPU v7x, 32 devices: a whole 2x2x4 slice. The times are simulated.
32 devices in a mesh: dap: 8 (over y, x, core), seq: 4 (over z).
Axes of the slice: x: 2, y: 2, z: 4, core: 2. Of those that a mesh axis runs over, the one named last changes fastest.
Arguments:
- homolog_tensor: bfloat16 [8, 32, 256], P('dap', 'seq'), may hold values from -6 to 6
- pair_features: bfloat16 [32, 32, 128], P('seq', 'dap'), may hold values from -6 to 6
- entry_real_mask: int32 [8, 32], P('dap', 'seq'), may hold values 0 or 1
- chain_ids: int32 [32], replicated, may hold values from 0 to 3, never falling along the last dimension, each value on 1 to 16 neighbouring positions
- horizontal_matrices: bfloat16 [256, 1024], replicated, may hold values from -0.375 to 0.375
- horizontal_projector: bfloat16 [256, 256], replicated, may hold values from -0.375 to 0.375
- bias_proj: float32 [128, 8], replicated, may hold values from -35.35534 to 35.35534
- chain_bias: float32 [2, 8], replicated, may hold values from -4 to 4
- column_proj: bfloat16 [256, 1024], replicated, may hold values from -12.5 to 12.5
- vertical_projector: bfloat16 [256, 256], replicated, may hold values from -0.375 to 0.375
- expansion_matrix: bfloat16 [256, 1024], replicated, may hold values from -0.375 to 0.375
- contraction_matrix: bfloat16 [1024, 256], replicated, may hold values from -0.1875 to 0.1875
Outputs:
- updated: bfloat16 [8, 32, 256], P('dap', 'seq')
Inputs may be any that keep to these rules, and one draw needn't show every extreme that they name: `chain_ids`: chain numbers never fall along the residues.
All inputs are finite; a program needn't handle non-finite values. No bound on the sum of `entry_real_mask` on one device may be relied on, other than what follows from the above.
Results may differ from a plain program's by a relative error of at most 0.013.
The roundings to bfloat16 on the way count: a program that leaves them out, or rounds other values in their place, can miss the bound.
Values may be sent and summed in bfloat16 or wider, within the bound.
No kernel may reach another device: no remote copies, remote signals or barrier semaphores. Data moves between devices by JAX's collectives and lax.ppermute only.
A program may use at most 64 MiB of HBM per device.

v0:
```python
import jax
import jax.numpy as jnp
from jax import lax
from jax.sharding import PartitionSpec as P

HEAD_TOTAL = 8
HEAD_DEPTH = 32
epsilon = 1e-05


def layer_norm(inputs):
    center = inputs - jnp.mean(inputs, axis=-1, keepdims=True)
    spread = jnp.mean(center * center, axis=-1, keepdims=True)
    return center * lax.rsqrt(spread + epsilon)


def attend(queries, key_part, value_part, keep_mask, bias_term):
    scores = jnp.einsum(
        "ihd,jhd->hij", queries, key_part, preferred_element_type=jnp.float32
    ) * HEAD_DEPTH ** (-0.5)
    if bias_term is not None:
        scores = scores + bias_term.astype(jnp.float32)
    scores = jnp.where(keep_mask[None, None, :] > 0, scores, -1000000000.0)
    weights = jax.nn.softmax(scores, axis=-1).astype(jnp.bfloat16)
    return jnp.einsum("hij,jhd->ihd", weights, value_part, preferred_element_type=jnp.float32)


def column_update(
    column, keep_column, column_proj, vertical_projector, expansion_matrix, contraction_matrix
):
    expanded_dimension = HEAD_TOTAL * HEAD_DEPTH
    standardized = layer_norm(column.astype(jnp.float32)).astype(jnp.bfloat16)
    projected = jnp.dot(standardized, column_proj, preferred_element_type=jnp.float32).astype(
        jnp.bfloat16
    )
    queries = projected[:, :expanded_dimension].reshape(-1, HEAD_TOTAL, HEAD_DEPTH)
    key_part = projected[:, expanded_dimension : 2 * expanded_dimension].reshape(
        -1, HEAD_TOTAL, HEAD_DEPTH
    )
    value_part = projected[:, 2 * expanded_dimension : 3 * expanded_dimension].reshape(
        -1, HEAD_TOTAL, HEAD_DEPTH
    )
    attended = attend(queries, key_part, value_part, keep_column, None).reshape(
        -1, expanded_dimension
    )
    sigmoid_scaled = (
        jax.nn.sigmoid(projected[:, 3 * expanded_dimension :].astype(jnp.float32)) * attended
    ).astype(jnp.bfloat16)
    mixed = column.astype(jnp.float32) + jnp.dot(
        sigmoid_scaled, vertical_projector, preferred_element_type=jnp.float32
    )
    inner = jnp.maximum(
        jnp.dot(
            layer_norm(mixed).astype(jnp.bfloat16),
            expansion_matrix,
            preferred_element_type=jnp.float32,
        ),
        0.0,
    ).astype(jnp.bfloat16)
    return (mixed + jnp.dot(inner, contraction_matrix, preferred_element_type=jnp.float32)).astype(
        jnp.bfloat16
    )


def body(
    homolog_tensor,
    pair_features,
    entry_real_mask,
    chain_ids,
    horizontal_matrices,
    horizontal_projector,
    bias_proj,
    chain_bias,
    column_proj,
    vertical_projector,
    expansion_matrix,
    contraction_matrix,
):
    row_count, local_residues, channels = homolog_tensor.shape
    expanded_dimension = HEAD_TOTAL * HEAD_DEPTH
    dap_count = lax.axis_size("dap")
    pair_rows, pair_columns, pair_width = pair_features.shape
    normed_pair = layer_norm(pair_features.astype(jnp.float32))
    projected_pair = jnp.einsum(
        "ijc,ch->hij", normed_pair, bias_proj, precision=lax.Precision.HIGHEST
    )
    row_chain = lax.dynamic_slice_in_dim(chain_ids, lax.axis_index("seq") * pair_rows, pair_rows)
    column_chain = lax.dynamic_slice_in_dim(
        chain_ids, lax.axis_index("dap") * pair_columns, pair_columns
    )
    same_chain = (row_chain[:, None] == column_chain[None, :]).astype(jnp.float32)
    chain_term = chain_bias[0][:, None, None] * same_chain + chain_bias[1][:, None, None] * (
        1.0 - same_chain
    )
    local_bias = (projected_pair + chain_term).astype(jnp.bfloat16)
    pair_bias = lax.all_gather(local_bias, "dap", axis=2, tiled=True)
    standardized = layer_norm(homolog_tensor.astype(jnp.float32)).astype(jnp.bfloat16)
    flat = standardized.reshape(-1, channels)
    keep_mask = entry_real_mask.astype(jnp.bfloat16)
    projected = (
        jnp.dot(flat, horizontal_matrices, preferred_element_type=jnp.float32)
        .astype(jnp.bfloat16)
        .reshape(row_count, local_residues, 4 * expanded_dimension)
    )
    queries = projected[..., :expanded_dimension]
    gating = projected[..., 3 * expanded_dimension :]
    key_values, keep_all = (
        lax.all_gather(
            projected[..., expanded_dimension : 3 * expanded_dimension], "seq", axis=1, tiled=True
        ),
        lax.all_gather(keep_mask, "seq", axis=1, tiled=True),
    )

    def one_row(inputs_row):
        row_queries, row_pairs, row_keep = inputs_row
        key_part = row_pairs[:, :expanded_dimension].reshape(-1, HEAD_TOTAL, HEAD_DEPTH)
        value_part = row_pairs[:, expanded_dimension:].reshape(-1, HEAD_TOTAL, HEAD_DEPTH)
        return attend(
            row_queries.reshape(local_residues, HEAD_TOTAL, HEAD_DEPTH),
            key_part,
            value_part,
            row_keep,
            pair_bias,
        ).reshape(local_residues, expanded_dimension)

    attended = lax.map(one_row, (queries, key_values, keep_all))
    sigmoid_scaled = (jax.nn.sigmoid(gating.astype(jnp.float32)) * attended).astype(jnp.bfloat16)
    row_result = jnp.dot(
        sigmoid_scaled.reshape(-1, expanded_dimension),
        horizontal_projector,
        preferred_element_type=jnp.float32,
    ).reshape(row_count, local_residues, channels)
    updated_rows = (homolog_tensor.astype(jnp.float32) + row_result).astype(jnp.bfloat16)
    per_device = local_residues // dap_count
    blocks = updated_rows.reshape(row_count, dap_count, per_device, channels)
    keep_blocks = keep_mask.reshape(row_count, dap_count, per_device)

    def single_column(inputs_col):
        return column_update(
            inputs_col[0],
            inputs_col[1],
            column_proj,
            vertical_projector,
            expansion_matrix,
            contraction_matrix,
        )

    column_block = lax.all_to_all(blocks, "dap", split_axis=1, concat_axis=0, tiled=True)
    column_keep = lax.all_to_all(keep_blocks, "dap", split_axis=1, concat_axis=0, tiled=True)
    inputs_col = (jnp.moveaxis(column_block[:, 0], 1, 0), jnp.moveaxis(column_keep[:, 0], 1, 0))
    output_list = lax.map(single_column, inputs_col)
    mixed = jnp.moveaxis(output_list, 0, 1)[:, None]
    returned = lax.all_to_all(mixed, "dap", split_axis=0, concat_axis=1, tiled=True)
    return returned.reshape(row_count, local_residues, channels)


def solution(mesh):
    placed = (
        P("dap", "seq", None),
        P("seq", "dap", None),
        P("dap", "seq"),
        P(),
        P(),
        P(),
        P(),
        P(),
        P(),
        P(),
        P(),
        P(),
    )
    return jax.shard_map(
        body, mesh=mesh, in_specs=placed, out_specs=P("dap", "seq", None), check_vma=False
    )
```

profile of v0, /device:TPU:0, one launch (start us, length us, event | category | flops | bytes accessed | tf_op | source)
XLA Modules:
  0.0 71.7 jit_solution(17577258312015481253)
XLA Ops:
  0.0 0.7 convert_bitcast_fusion.1
  0.7 0.7 copy.49
  1.4 5.2 %all-to-all-start.1 = ((bf16[1,8,1]{2,0,1:T(2,128)(2,1)}), bf16[1,8,1]{2,0,1:T(2,128)(2,1)S(1)}, u32[]{:S(2)}, u32[]{:S(2)}) async-start(bf16[1,8,1]{2,0,1:T(2,128)(2,1)} %copy.49), calls=%async_computation.1 | async-start | bytes 8192 | tf_op jit(solution)/shard_map/all_to_all | solution.py:149
  6.6 0.7 copy-done.12
  7.3 0.1 dynamic_slice.21
  7.3 0.1 dynamic_slice.20
  7.4 0.1 broadcast_subtract_fusion
  7.5 0.1 compare_convert_fusion
  7.6 0.5 copy-done.6
  8.0 0.1 convert_reduce_fusion.1
  8.1 0.2 fusion.38
  8.3 0.2 fusion.12
  8.6 0.6 copy-done.7
  9.2 0.7 copy-done.5
  9.9 0.1 convert_reduce_fusion
  10.0 0.2 fusion.24
  10.1 0.0 copy-start.9
  10.1 0.1 fusion.22
  10.2 0.6 copy-done.9
  10.8 0.7 copy-done.11
  11.5 0.1 fusion.13
  11.6 0.1 copy.43
  11.7 9.7 %all_gather.11 = bf16[8,8,32]{1,0,2:T(8,128)(2,1)S(1)} all-gather(bf16[8,8,4]{1,0,2:T(8,128)(2,1)S(1)} %copy.43), channel_id=1, replica_groups=mesh['dap'=8,'seq'=4] {'dap'}, dimensions={2}, use_global_device_ids=true | all-gather | bytes 4608 | tf_op jit(solution)/shard_map/all_gather | solution.py:96
  21.5 0.1 copy.44
  21.6 0.6 slice-done
  22.2 13.4 %all_gather.9 = bf16[1,32,512]{2,1,0:T(8,128)(2,1)S(1)} all-gather(bf16[1,8,512]{2,1,0:T(8,128)(2,1)S(1)} %slice-done), channel_id=1, replica_groups=mesh['dap'=8,'seq'=4] {'seq'}, dimensions={1}, use_global_device_ids=true | all-gather | bytes 40960 | tf_op jit(solution)/shard_map/all_gather | solution.py:108
  35.6 0.1 reshape.208
  35.7 0.6 slice-done.1
  36.2 0.1 reshape.207
  36.3 0.6 dynamic-slice
  37.6 0.2 dynamic-update-slice
  37.8 11.7 %all-reduce = bf16[32]{0:T(256)(128)(2,1)S(1)} all-reduce(bf16[32]{0:T(256)(128)(2,1)S(1)} %dynamic-update-slice), channel_id=1, replica_groups=mesh['dap'=8,'seq'=4] {'seq'}, use_global_device_ids=true, to_apply=%add | all-reduce | flops 32 | bytes 128
  49.5 0.1 fusion.8
  49.7 0.2 fusion.66
  49.9 0.1 reshape.206
  50.0 0.0 copy-start.3
  50.0 0.3 convolution_bitcast_fusion.1
  50.3 0.1 broadcast_in_dim.72
  50.3 0.5 copy-done.3
  50.9 0.1 copy-done.8
  51.0 0.1 fusion.19
  51.2 0.6 broadcast.220
  51.8 0.7 %reduce.5 = bf16[8,256]{1,0:T(8,128)(2,1)S(1)} reduce(bf16[8,1,1,256]{3,2,1,0:T(2,128)(2,1)S(1)} %bitcast.75, bf16[]{:T(256)} %broadcast.220), dimensions={1,2}, to_apply=%bitcast.73.reduce_sub_computation | reduce | bytes 8194
  52.5 0.6 reshape.228
  53.1 3.3 %all-to-all-start = ((bf16[8,2,128]{2,1,0:T(2,128)(2,1)}), bf16[8,2,128]{2,1,0:T(2,128)(2,1)S(1)}, u32[]{:S(2)}, u32[]{:S(2)}) async-start(bf16[8,2,128]{2,1,0:T(2,128)(2,1)} %reshape.228), calls=%async_computation | async-start | bytes 8192 | tf_op jit(solution)/shard_map/all_to_all | solution.py:148
  56.4 0.2 compare_reduce_fusion
  56.6 4.3 %all-to-all-done = bf16[8,2,128]{2,1,0:T(2,128)(2,1)S(1)} async-done(((bf16[8,2,128]{2,1,0:T(2,128)(2,1)}), bf16[8,2,128]{2,1,0:T(2,128)(2,1)S(1)}, u32[]{:S(2)}, u32[]{:S(2)}) %all-to-all-start) | async-done | bytes 4128 | tf_op jit(solution)/shard_map/all_to_all | solution.py:148
  61.0 0.1 convert_reduce_fusion.2
  61.1 0.2 fusion.40
  61.3 0.0 copy-start.4
  61.3 0.2 convolution_convert_fusion
  61.5 0.1 reshape.214
  61.6 0.1 reshape.215
  61.7 0.1 fusion.6
  61.8 0.2 fusion.67
  62.0 0.1 reshape.212
  62.1 0.2 convolution_bitcast_fusion
  62.3 0.1 reshape.216
  62.4 0.3 fusion.72
  62.7 0.2 multiply_reduce_fusion
  62.9 0.4 fusion.18
  63.3 0.7 reduce.6
  64.0 7.1 %all_to_all.12 = bf16[8,2,128]{2,1,0:T(2,128)(2,1)S(1)} all-to-all(bf16[8,2,128]{2,1,0:T(2,128)(2,1)S(1)} %reshape.230), channel_id=1, replica_groups=mesh['dap'=8,'seq'=4] {'dap'}, dimensions={0} | all-to-all | bytes 8192 | tf_op jit(solution)/shard_map/all_to_all | solution.py:153
  71.1 0.6 copy.83
  (39 shorter events, 0.2 us)
Async XLA Ops:
  0.0 8.3 %copy-start = (bf16[256,1024]{1,0:T(8,128)(2,1)S(1)}, bf16[256,1024]{1,0:T(8,128)(2,1)}, u32[]{:S(2)}) copy-start(bf16[256,1024]{1,0:T(8,128)(2,1)} %param.16) | copy-start | bytes 1572868
  1.4 51.7 %all-to-all-start.1 = ((bf16[1,8,1]{2,0,1:T(2,128)(2,1)}), bf16[1,8,1]{2,0,1:T(2,128)(2,1)S(1)}, u32[]{:S(2)}, u32[]{:S(2)}) async-start(bf16[1,8,1]{2,0,1:T(2,128)(2,1)} %copy.49), calls=%async_computation.1 | async-start | bytes 8192 | tf_op jit(solution)/shard_map/all_to_all | solution.py:149
  6.6 0.7 copy-start.12
  7.3 0.7 copy-start.6
  8.6 0.6 copy-start.7
  9.2 0.7 copy-start.5
  10.1 0.7 copy-start.9
  10.8 0.7 copy-start.11
  21.5 0.7 slice-start
  35.5 0.8 %copy-start.13 = (u32[32]{0:T(128)S(1)}, u32[32]{0:T(128)}, u32[]{:S(2)}) copy-start(u32[32]{0:T(128)} %constant.98) | copy-start | bytes 388
  35.5 0.7 slice-start.1
  35.5 25.7 %copy-start.10 = (bf16[256,1024]{1,0:T(8,128)(2,1)S(1)}, bf16[256,1024]{1,0:T(8,128)(2,1)}, u32[]{:S(2)}) copy-start(bf16[256,1024]{1,0:T(8,128)(2,1)} %param.20) | copy-start | bytes 1572868
  50.0 0.9 %copy-start.3 = (bf16[256,256]{1,0:T(8,128)(2,1)S(1)}, bf16[256,256]{1,0:T(8,128)(2,1)}, u32[]{:S(2)}) copy-start(bf16[256,256]{1,0:T(8,128)(2,1)} %param.17) | copy-start | bytes 393220
  50.3 0.7 %copy-start.8 = (bf16[1,8,1024]{2,1,0:T(8,128)(2,1)S(1)}, bf16[1,8,1024]{2,1,0:T(8,128)(2,1)}, u32[]{:S(2)}) copy-start(bf16[1,8,1024]{2,1,0:T(8,128)(2,1)} %copy-done.7) | copy-start | bytes 49156
  53.1 7.9 %all-to-all-start = ((bf16[8,2,128]{2,1,0:T(2,128)(2,1)}), bf16[8,2,128]{2,1,0:T(2,128)(2,1)S(1)}, u32[]{:S(2)}, u32[]{:S(2)}) async-start(bf16[8,2,128]{2,1,0:T(2,128)(2,1)} %reshape.228), calls=%async_computation | async-start | bytes 8192 | tf_op jit(solution)/shard_map/all_to_all | solution.py:148
  61.3 1.1 %copy-start.4 = (bf16[256,256]{1,0:T(8,128)(2,1)S(1)}, bf16[256,256]{1,0:T(8,128)(2,1)}, u32[]{:S(2)}) copy-start(bf16[256,256]{1,0:T(8,128)(2,1)} %param.21) | copy-start | bytes 393220
  61.3 1.6 %copy-start.2 = (bf16[256,1024]{1,0:T(8,128)(2,1)S(1)}, bf16[256,1024]{1,0:T(8,128)(2,1)}, u32[]{:S(2)}) copy-start(bf16[256,1024]{1,0:T(8,128)(2,1)} %param.22) | copy-start | bytes 1572868
  61.5 1.3 %copy-start.1 = (bf16[1024,256]{1,0:T(8,128)(2,1)S(1)}, bf16[1024,256]{1,0:T(8,128)(2,1)}, u32[]{:S(2)}) copy-start(bf16[1024,256]{1,0:T(8,128)(2,1)} %param.23) | copy-start | bytes 1572868
where the time goes:
time: 72.2 us; the launch traced here: 71.7 us
  blocking collectives  41.9 us (58%)
  local copies, waits for them, and re-layouts  9.98 us (14%)
  starting transfers between devices  8.51 us (12%)
  waiting for transfers between devices  4.3 us (6%)
  other arithmetic  3.88 us (5%)
  matrix products  2.23 us (3%)
  between operations  0.87 us (1%)
    all_gather x1, blocking collectives, body(): lax.all_gather(projected[..., expanded_dimension:3 * expanded_dimension],...  13.4 us
    unnamed x1, blocking collectives  11.7 us
    all_gather x1, blocking collectives, body(): pair_bias = lax.all_gather(local_bias, 'dap', axis=2, tiled=True)  9.75 us
    all_to_all x1, blocking collectives, body(): lax.all_to_all(mixed, 'dap', split_axis=0, concat_axis=1, tiled=True)  7.05 us
    unnamed x37, local copies, waits for them, and re-layouts  7.04 us
    all_to_all x1, starting transfers between devices, body(): lax.all_to_all(keep_blocks, 'dap', split_axis=1, concat_axis=0, tiled=True)  5.2 us
    all_to_all x1, waiting for transfers between devices, body(): lax.all_to_all(blocks, 'dap', split_axis=1, concat_axis=0, tiled=True)  4.3 us
    all_to_all x1, starting transfers between devices, body(): lax.all_to_all(blocks, 'dap', split_axis=1, concat_axis=0, tiled=True)  3.31 us
  transfers between devices with their start and end apart: 2, of which 1 were waited for; matrix products, arithmetic and copies ran while one was open for 8% of the time, Pallas kernels for 0%

commit v1 on v0

--- a/solution.py
+++ b/solution.py
@@ -6,6 +6,19 @@
 HEAD_TOTAL = 8
 HEAD_DEPTH = 32
 epsilon = 1e-05
+
+
+def ring_gather(value, axis, dim):
+    ways = lax.axis_size(axis)
+    up = [(d, (d + 1) % ways) for d in range(ways)]
+    down = [(d, (d - 1) % ways) for d in range(ways)]
+    earlier, later = ([value], [value])
+    for _ in range(ways // 2):
+        earlier.append(lax.ppermute(earlier[-1], axis, up))
+    for _ in range((ways - 1) // 2):
+        later.append(lax.ppermute(later[-1], axis, down))
+    line = jnp.concatenate([*earlier[::-1], *later[1:]], axis=dim)
+    return jnp.roll(line, (lax.axis_index(axis) - ways // 2) * value.shape[dim], axis=dim)
 
 
 def layer_norm(inputs):
@@ -105,9 +118,7 @@
     queries = projected[..., :expanded_dimension]
     gating = projected[..., 3 * expanded_dimension :]
     key_values, keep_all = (
-        lax.all_gather(
-            projected[..., expanded_dimension : 3 * expanded_dimension], "seq", axis=1, tiled=True
-        ),
+        ring_gather(projected[..., expanded_dimension : 3 * expanded_dimension], "seq", 1),
         lax.all_gather(keep_mask, "seq", axis=1, tiled=True),
     )
 

time: 72.2 us -> 60.4 us (0.84)
  blocking collectives: 41.9 us -> 26.9 us
  starting transfers between devices: 8.51 us -> 12.6 us
  local copies, waits for them, and re-layouts: 9.98 us -> 8.95 us
    all_gather x1 -> x0, blocking collectives: 13.4 us -> none  [body(): lax.all_gather(projected[..., expanded_dimension:3 * expanded_dimension],...]
    ppermute x0 -> x3, starting transfers between devices: none -> 5.41 us  [the longest x2 3.32 us: ring_gather(): earlier.append(lax.ppermute(earlier[-1], axis, up))]
    unnamed x1, blocking collectives: 11.7 us -> 10.1 us
    all_to_all x1, starting transfers between devices: 5.2 us -> 3.88 us  [body(): lax.all_to_all(keep_blocks, 'dap', split_axis=1, concat_axis=0, tiled=True)]
    reduce_sum x3, other arithmetic: 0.31 us -> 1.07 us  [layer_norm(): center = inputs - jnp.mean(inputs, axis=-1, keepdims=True)]
    unnamed x37 -> x46, local copies, waits for them, and re-layouts: 7.04 us -> 6.57 us
  transfers between devices with their start and end apart: 2 -> 5, of which waited for: 1 -> 1; matrix products, arithmetic and copies ran while one was open for 8% -> 10% of each run, Pallas kernels for 0% -> 0%
where the time goes in v1:
time: 60.4 us; the launch traced here: 59.9 us
  blocking collectives  26.9 us (45%)
  starting transfers between devices  12.6 us (21%)
  local copies, waits for them, and re-layouts  8.95 us (15%)
  waiting for transfers between devices  4.31 us (7%)
  other arithmetic  3.83 us (6%)
  matrix products  2.34 us (4%)
  between operations  0.93 us (2%)
    unnamed x1, blocking collectives  10.1 us
    all_gather x1, blocking collectives, body(): pair_bias = lax.all_gather(local_bias, 'dap', axis=2, tiled=True)  9.75 us
    all_to_all x1, blocking collectives, body(): lax.all_to_all(mixed, 'dap', split_axis=0, concat_axis=1, tiled=True)  7.05 us
    unnamed x46, local copies, waits for them, and re-layouts  6.57 us
    all_to_all x1, waiting for transfers between devices, body(): lax.all_to_all(blocks, 'dap', split_axis=1, concat_axis=0, tiled=True)  4.3 us
    all_to_all x1, starting transfers between devices, body(): lax.all_to_all(keep_blocks, 'dap', split_axis=1, concat_axis=0, tiled=True)  3.88 us
    ppermute x2, starting transfers between devices, ring_gather(): earlier.append(lax.ppermute(earlier[-1], axis, up))  3.32 us
    all_to_all x1, starting transfers between devices, body(): lax.all_to_all(blocks, 'dap', split_axis=1, concat_axis=0, tiled=True)  3.31 us
  transfers between devices with their start and end apart: 5, of which 1 were waited for; matrix products, arithmetic and copies ran while one was open for 10% of the time, Pallas kernels for 0%

profile of v1, /device:TPU:0, one launch (start us, length us, event | category | flops | bytes accessed | tf_op | source)
XLA Modules:
  0.0 59.9 jit_solution(10465568497459434872)
XLA Ops:
  0.0 0.9 %convert_reduce_fusion.1 = f32[8]{0:T(128)S(1)} fusion(bf16[1,8,256]{2,1,0:T(8,128)(2,1)} %param.12), kind=kLoop, calls=%fused_computation.57 | loop fusion | flops 4088 | bytes 4128 | tf_op jit(solution)/shard_map/reduce_sum | solution.py:25
  0.9 0.2 fusion.38
  1.1 0.2 fusion.12
  1.3 3.1 %collective-permute-start = (bf16[1,8,512]{2,1,0:T(8,128)(2,1)S(1)}, bf16[1,8,512]{2,1,0:T(8,128)(2,1)S(1)}, u32[]{:S(2)}, u32[]{:S(2)}) collective-permute-start(bf16[1,8,512]{2,1,0:T(8,128)(2,1)S(1)} %slice.51), channel_id=1, source_target_pairs={{0,1},{1,2},{2,3},{3,0},{4,5},{5,6},{6,7},{7,4},{8,9},{9,10},{10,1... | collective-permute-start | bytes 24584 | tf_op jit(solution)/shard_map/ppermute | solution.py:17
  4.4 2.1 %collective-permute-start.2 = (bf16[1,8,512]{2,1,0:T(8,128)(2,1)S(1)}, bf16[1,8,512]{2,1,0:T(8,128)(2,1)S(1)}, u32[]{:S(2)}, u32[]{:S(2)}) collective-permute-start(bf16[1,8,512]{2,1,0:T(8,128)(2,1)S(1)} %slice.51), channel_id=1, source_target_pairs={{0,3},{1,0},{2,1},{3,2},{4,7},{5,4},{6,5},{7,6},{8,11},{9,8},{10,9... | collective-permute-start | bytes 24584 | tf_op jit(solution)/shard_map/ppermute | solution.py:19
  6.5 0.7 %copy.56 = bf16[1,8,1]{2,0,1:T(2,128)(2,1)} copy(bf16[1,8,1]{1,2,0:T(2,128)(2,1)S(1)} %get-tuple-element.46) | data formatting | bytes 32 | tf_op jit(solution)/shard_map/reshape | solution.py:147
  7.2 3.9 %all-to-all-start.1 = ((bf16[1,8,1]{2,0,1:T(2,128)(2,1)}), bf16[1,8,1]{2,0,1:T(2,128)(2,1)S(1)}, u32[]{:S(2)}, u32[]{:S(2)}) async-start(bf16[1,8,1]{2,0,1:T(2,128)(2,1)} %copy.56), calls=%async_computation.1 | async-start | bytes 8192 | tf_op jit(solution)/shard_map/all_to_all | solution.py:160
  11.1 0.0 copy-start.13
  11.1 0.7 %copy-done.13 = s32[32]{0:T(128)S(1)} copy-done((s32[32]{0:T(128)S(1)}, s32[32]{0:T(128)}, u32[]{:S(2)}) %copy-start.13) | copy-done | bytes 152
  11.7 0.1 dynamic_slice.25
  11.8 0.1 dynamic_slice.26
  11.9 0.1 convert_reduce_fusion
  12.0 0.2 fusion.24
  12.1 0.1 compare_convert_fusion
  12.2 0.1 add_rsqrt_fusion
  12.3 0.6 %copy-done.9 = f32[2,8]{1,0:T(2,128)S(1)} copy-done((f32[2,8]{1,0:T(2,128)S(1)}, f32[2,8]{1,0:T(2,128)}, u32[]{:S(2)}) %copy-start.9) | copy-done | bytes 88
  12.9 0.7 %copy-done.11 = f32[128,8]{0,1:T(8,128)S(1)} copy-done((f32[128,8]{0,1:T(8,128)S(1)}, f32[128,8]{0,1:T(8,128)}, u32[]{:S(2)}) %copy-start.11) | copy-done | bytes 4120
  13.6 0.2 fusion.13
  13.8 0.0 copy-start.14
  13.9 0.6 %copy-done.14 = u32[32]{0:T(128)S(1)} copy-done((u32[32]{0:T(128)S(1)}, u32[32]{0:T(128)}, u32[]{:S(2)}) %copy-start.14) | copy-done | bytes 152
  14.5 0.6 dynamic-slice
  15.8 0.2 dynamic-update-slice
  16.0 10.1 %all-reduce = bf16[32]{0:T(256)(128)(2,1)S(1)} all-reduce(bf16[32]{0:T(256)(128)(2,1)S(1)} %dynamic-update-slice), channel_id=1, replica_groups=mesh['dap'=8,'seq'=4] {'seq'}, use_global_device_ids=true, to_apply=%add | all-reduce | flops 32 | bytes 128
  26.1 0.2 collective-permute-start.1
  26.4 0.1 copy.50
  26.5 9.7 %all_gather.7 = bf16[8,8,32]{1,0,2:T(8,128)(2,1)S(1)} all-gather(bf16[8,8,4]{1,0,2:T(8,128)(2,1)S(1)} %copy.50), channel_id=1, replica_groups=mesh['dap'=8,'seq'=4] {'dap'}, dimensions={2}, use_global_device_ids=true | all-gather | bytes 4608 | tf_op jit(solution)/shard_map/all_gather | solution.py:109
  36.2 0.1 copy.51
  36.3 0.6 slice-done
  36.9 0.1 reshape.207
  37.0 0.7 %copy-done.6 = bf16[1,8,1024]{2,1,0:T(8,128)(2,1)S(1)} copy-done((bf16[1,8,1024]{2,1,0:T(8,128)(2,1)S(1)}, bf16[1,8,1024]{2,1,0:T(8,128)(2,1)}, u32[]{:S(2)}) %copy-start.6) | copy-done | bytes 16408
  37.7 0.0 copy-start.10
  37.8 0.1 reshape.208
  37.9 0.1 fusion.8
  38.0 0.2 fusion.68
  38.2 0.1 reshape.206
  38.3 0.0 copy-start.3
  38.3 0.3 convolution_bitcast_fusion.1
  38.6 0.1 broadcast_in_dim.72
  38.7 0.5 copy-done.3
  39.2 0.1 fusion.19
  39.4 0.6 broadcast.221
  40.0 0.7 %reduce.5 = bf16[8,256]{1,0:T(8,128)(2,1)S(1)} reduce(bf16[8,1,1,256]{3,2,1,0:T(2,128)(2,1)S(1)} %bitcast.75, bf16[]{:T(256)} %broadcast.221), dimensions={1,2}, to_apply=%bitcast.74.reduce_sub_computation | reduce | bytes 8194
  40.7 0.6 %reshape.228 = bf16[8,2,128]{2,1,0:T(2,128)(2,1)} reshape(bf16[8,256]{1,0:T(8,128)(2,1)S(1)} %reduce.5) | data formatting | bytes 8192
  41.3 3.3 %all-to-all-start = ((bf16[8,2,128]{2,1,0:T(2,128)(2,1)}), bf16[8,2,128]{2,1,0:T(2,128)(2,1)S(1)}, u32[]{:S(2)}, u32[]{:S(2)}) async-start(bf16[8,2,128]{2,1,0:T(2,128)(2,1)} %reshape.228), calls=%async_computation | async-start | bytes 8192 | tf_op jit(solution)/shard_map/all_to_all | solution.py:159
  44.6 0.2 compare_reduce_fusion
  44.9 4.3 %all-to-all-done = bf16[8,2,128]{2,1,0:T(2,128)(2,1)S(1)} async-done(((bf16[8,2,128]{2,1,0:T(2,128)(2,1)}), bf16[8,2,128]{2,1,0:T(2,128)(2,1)S(1)}, u32[]{:S(2)}, u32[]{:S(2)}) %all-to-all-start) | async-done | bytes 4128 | tf_op jit(solution)/shard_map/all_to_all | solution.py:159
  49.2 0.1 convert_reduce_fusion.2
  49.3 0.2 fusion.40
  49.5 0.0 copy-start.4
  49.5 0.0 copy-start.2
  49.5 0.2 convolution_convert_fusion
  49.8 0.1 reshape.214
  49.9 0.1 reshape.215
  49.9 0.1 fusion.6
  50.1 0.2 fusion.69
  50.2 0.1 reshape.212
  50.3 0.2 convolution_bitcast_fusion
  50.5 0.1 reshape.216
  50.6 0.3 fusion.74
  50.9 0.2 multiply_reduce_fusion
  51.1 0.4 fusion.18
  51.5 0.7 %reduce.6 = bf16[8,256]{1,0:T(8,128)(2,1)S(1)} reduce(bf16[8,1,1,256]{3,0,2,1:T(8,128)(2,1)S(1)} %fusion.18, bf16[]{:T(256)} %broadcast.221), dimensions={1,2}, to_apply=%copy.62.reduce_sub_computation | reduce | bytes 8194 | tf_op jit(solution)/shard_map/broadcast_in_dim;transpose | solution.py:163
  52.2 7.1 %all_to_all.12 = bf16[8,2,128]{2,1,0:T(2,128)(2,1)S(1)} all-to-all(bf16[8,2,128]{2,1,0:T(2,128)(2,1)S(1)} %reshape.230), channel_id=1, replica_groups=mesh['dap'=8,'seq'=4] {'dap'}, dimensions={0} | all-to-all | bytes 8192 | tf_op jit(solution)/shard_map/all_to_all | solution.py:164
  59.3 0.6 %copy.88 = bf16[8,1,1,256]{3,0,1,2:T(8,128)(2,1)} copy(bf16[8,1,1,256]{3,2,1,0:T(2,128)(2,1)S(1)} %reshape.231) | data formatting | bytes 8192
  (52 shorter events, 0.2 us)
Async XLA Ops:
  0.0 1.1 %copy-start = (bf16[256,1024]{1,0:T(8,128)(2,1)S(1)}, bf16[256,1024]{1,0:T(8,128)(2,1)}, u32[]{:S(2)}) copy-start(bf16[256,1024]{1,0:T(8,128)(2,1)} %param.16) | copy-start | bytes 1572868
  0.0 0.9 %copy-start.7 = (bf16[1,8,256]{2,1,0:T(8,128)(2,1)S(1)}, bf16[1,8,256]{2,1,0:T(8,128)(2,1)}, u32[]{:S(2)}) copy-start(bf16[1,8,256]{2,1,0:T(8,128)(2,1)} %param.12) | copy-start | bytes 12292
  1.3 25.1 %copy-start.5 = (bf16[1,8,1024]{2,1,0:T(8,128)(2,1)}, bf16[1,8,1024]{2,1,0:T(8,128)(2,1)S(1)}, u32[]{:S(2)}) copy-start(bf16[1,8,1024]{2,1,0:T(8,128)(2,1)S(1)} %fusion.12) | copy-start | bytes 49156
  1.3 5.2 %copy-start.12 = (s32[1,8]{1,0:T(1,128)S(1)}, s32[1,8]{1,0:T(1,128)}, u32[]{:S(2)}) copy-start(s32[1,8]{1,0:T(1,128)} %param.14) | copy-start | bytes 100
  1.3 24.8 %collective-permute-start = (bf16[1,8,512]{2,1,0:T(8,128)(2,1)S(1)}, bf16[1,8,512]{2,1,0:T(8,128)(2,1)S(1)}, u32[]{:S(2)}, u32[]{:S(2)}) collective-permute-start(bf16[1,8,512]{2,1,0:T(8,128)(2,1)S(1)} %slice.51), channel_id=1, source_target_pairs={{0,1},{1,2},{2,3},{3,0},{4,5},{5,6},{6,7},{7,4},{8,9},{9,10},{10,1... | collective-permute-start | bytes 24584 | tf_op jit(solution)/shard_map/ppermute | solution.py:17
  4.4 33.3 %collective-permute-start.2 = (bf16[1,8,512]{2,1,0:T(8,128)(2,1)S(1)}, bf16[1,8,512]{2,1,0:T(8,128)(2,1)S(1)}, u32[]{:S(2)}, u32[]{:S(2)}) collective-permute-start(bf16[1,8,512]{2,1,0:T(8,128)(2,1)S(1)} %slice.51), channel_id=1, source_target_pairs={{0,3},{1,0},{2,1},{3,2},{4,7},{5,4},{6,5},{7,6},{8,11},{9,8},{10,9... | collective-permute-start | bytes 24584 | tf_op jit(solution)/shard_map/ppermute | solution.py:19
  7.2 34.1 %all-to-all-start.1 = ((bf16[1,8,1]{2,0,1:T(2,128)(2,1)}), bf16[1,8,1]{2,0,1:T(2,128)(2,1)S(1)}, u32[]{:S(2)}, u32[]{:S(2)}) async-start(bf16[1,8,1]{2,0,1:T(2,128)(2,1)} %copy.56), calls=%async_computation.1 | async-start | bytes 8192 | tf_op jit(solution)/shard_map/all_to_all | solution.py:160
  11.1 0.8 %copy-start.8 = (bf16[8,4,128]{2,1,0:T(4,128)(2,1)S(1)}, bf16[8,4,128]{2,1,0:T(4,128)(2,1)}, u32[]{:S(2)}) copy-start(bf16[8,4,128]{2,1,0:T(4,128)(2,1)} %param.13) | copy-start | bytes 24580
  11.1 0.7 %copy-start.13 = (s32[32]{0:T(128)S(1)}, s32[32]{0:T(128)}, u32[]{:S(2)}) copy-start(s32[32]{0:T(128)} %param.15) | copy-start | bytes 388
  12.2 0.7 %copy-start.9 = (f32[2,8]{1,0:T(2,128)S(1)}, f32[2,8]{1,0:T(2,128)}, u32[]{:S(2)}) copy-start(f32[2,8]{1,0:T(2,128)} %param.19) | copy-start | bytes 196
  12.9 0.7 %copy-start.11 = (f32[128,8]{0,1:T(8,128)S(1)}, f32[128,8]{0,1:T(8,128)}, u32[]{:S(2)}) copy-start(f32[128,8]{0,1:T(8,128)} %param.18) | copy-start | bytes 12292
  13.8 0.7 %copy-start.14 = (u32[32]{0:T(128)S(1)}, u32[32]{0:T(128)}, u32[]{:S(2)}) copy-start(u32[32]{0:T(128)} %constant.121) | copy-start | bytes 388
  26.1 10.8 %collective-permute-start.1 = (bf16[1,8,512]{2,1,0:T(8,128)(2,1)S(1)}, bf16[1,8,512]{2,1,0:T(8,128)(2,1)S(1)}, u32[]{:S(2)}, u32[]{:S(2)}) collective-permute-start(bf16[1,8,512]{2,1,0:T(8,128)(2,1)S(1)} %collective-permute-done), channel_id=1, source_target_pairs={{0,1},{1,2},{2,3},{3,0},{4,5},{5,6},{6,7},{7,4},{8,9},{9,10},{10,1... | collective-permute-start | bytes 24584 | tf_op jit(solution)/shard_map/ppermute | solution.py:17
  36.2 0.7 %slice-start = ((bf16[1,8,1024]{2,1,0:T(8,128)(2,1)}), bf16[1,8,256]{2,1,0:T(8,128)(2,1)S(1)}, s32[]{:S(2)}) async-start(bf16[1,8,1024]{2,1,0:T(8,128)(2,1)} %copy-done.5), calls=%async_computation.3 | async-start | bytes 8192 | tf_op jit(solution)/shard_map/slice | solution.py:118
  37.0 0.7 %copy-start.6 = (bf16[1,8,1024]{2,1,0:T(8,128)(2,1)S(1)}, bf16[1,8,1024]{2,1,0:T(8,128)(2,1)}, u32[]{:S(2)}) copy-start(bf16[1,8,1024]{2,1,0:T(8,128)(2,1)} %copy-done.5) | copy-start | bytes 49156
  37.7 11.8 %copy-start.10 = (bf16[256,1024]{1,0:T(8,128)(2,1)S(1)}, bf16[256,1024]{1,0:T(8,128)(2,1)}, u32[]{:S(2)}) copy-start(bf16[256,1024]{1,0:T(8,128)(2,1)} %param.20) | copy-start | bytes 1572868
  38.3 0.9 %copy-start.3 = (bf16[256,256]{1,0:T(8,128)(2,1)S(1)}, bf16[256,256]{1,0:T(8,128)(2,1)}, u32[]{:S(2)}) copy-start(bf16[256,256]{1,0:T(8,128)(2,1)} %param.17) | copy-start | bytes 393220
  41.3 7.9 %all-to-all-start = ((bf16[8,2,128]{2,1,0:T(2,128)(2,1)}), bf16[8,2,128]{2,1,0:T(2,128)(2,1)S(1)}, u32[]{:S(2)}, u32[]{:S(2)}) async-start(bf16[8,2,128]{2,1,0:T(2,128)(2,1)} %reshape.228), calls=%async_computation | async-start | bytes 8192 | tf_op jit(solution)/shard_map/all_to_all | solution.py:159
  49.5 1.1 %copy-start.4 = (bf16[256,256]{1,0:T(8,128)(2,1)S(1)}, bf16[256,256]{1,0:T(8,128)(2,1)}, u32[]{:S(2)}) copy-start(bf16[256,256]{1,0:T(8,128)(2,1)} %param.21) | copy-start | bytes 393220
  49.5 1.6 %copy-start.2 = (bf16[256,1024]{1,0:T(8,128)(2,1)S(1)}, bf16[256,1024]{1,0:T(8,128)(2,1)}, u32[]{:S(2)}) copy-start(bf16[256,1024]{1,0:T(8,128)(2,1)} %param.22) | copy-start | bytes 1572868
  49.8 1.3 %copy-start.1 = (bf16[1024,256]{1,0:T(8,128)(2,1)S(1)}, bf16[1024,256]{1,0:T(8,128)(2,1)}, u32[]{:S(2)}) copy-start(bf16[1024,256]{1,0:T(8,128)(2,1)} %param.23) | copy-start | bytes 1572868
